TPU v7x, 512 devices: a whole 4x8x8 slice. The times are simulated.
512 devices in a mesh: section: 16 (over x, z_hi), tensor: 32 (over y, z_lo, core).
Axes of the slice: x: 4, y: 8, z: 8 (z_hi: 4, z_lo: 2; z = z_hi * 2 + z_lo), core: 2. Of those that a mesh axis runs over, the one named last changes fastest.
Arguments:
- x_in: bfloat16 [16, 512, 4096], P('section', 'tensor'), may hold values from -40 to 40
- grad_out: bfloat16 [16, 512, 4096], P('section', 'tensor'), may hold values from -50 to 50
- gain: float32 [16, 4096], P('section'), may hold values from 0.5 to 1.5
- w_val: bfloat16 [16, 4096, 4096], P('section', 'tensor'), may hold values from -0.09375 to 0.09375
- w_out: bfloat16 [16, 4096, 4096], P('section', 'tensor'), may hold values from -0.09375 to 0.09375
- filt: float32 [16, 3, 4096], P('section', None, 'tensor'), may hold values from -3 to 3
- tail: bfloat16 [16, 2, 4096], P('section', None, 'tensor'), may hold values from -6 to 6
- micro_index: int32 [16], P('section'), may hold values from 0 to 15
Outputs:
- grad_in: bfloat16 [16, 512, 4096], P('section', 'tensor')
- grad_w_val: bfloat16 [16, 4096, 4096], P('section', 'tensor')
- grad_w_out: bfloat16 [16, 4096, 4096], P('section', 'tensor')
- grad_filter: float32 [16, 3, 4096], P('section', None, 'tensor')
- grad_tail: float32 [16, 2, 4096], P('section', None, 'tensor')
- grad_gain: float32 [16, 4096], P('section')
All inputs are finite; a program needn't handle non-finite values.
Results may differ from a plain program's by a relative error of at most 0.023.
Values may be sent and summed in bfloat16 or wider, within the bound.
No kernel may reach another device: no remote copies, remote signals or barrier semaphores. Data moves between devices by JAX's collectives and lax.ppermute only.
A program may use at most 64 MiB of HBM per device.

v0:
```python
import jax
import jax.numpy as jnp
from jax import lax
from jax.sharding import PartitionSpec as P

TAPS = 3
EPSILON = 1e-06


def shifted(block, axis, distance):
    devices = range(lax.axis_size(axis))
    route = [((i - distance) % len(devices), i) for i in devices]
    return lax.ppermute(block, axis, route)


def contract_last(left, right):
    return lax.dot_general(
        left, right, (((1,), (1,)), ((), ())), preferred_element_type=jnp.float32
    )


def contract_first(left, right):
    return lax.dot_general(
        left, right, (((0,), (0,)), ((), ())), preferred_element_type=jnp.float32
    )


def on_device(x_in, grad_out, gain, w_val, w_out, filt, tail, micro_index):
    x_rows = x_in[0]
    cot_rows = grad_out[0]
    gain_row = gain[0]
    val_weight = w_val[0]
    out_weight = w_out[0]
    filters = filt[0]
    tail_rows = tail[0]
    has_tail = micro_index[0] > 0
    x_float = x_rows.astype(jnp.float32)
    inv_rms = lax.rsqrt(jnp.mean(x_float * x_float, axis=-1, keepdims=True) + EPSILON)
    normed = (x_float * inv_rms * gain_row).astype(jnp.bfloat16)
    normed_all = lax.all_gather(normed, "tensor", axis=0, tiled=True)
    seq_len = normed_all.shape[0]
    values = contract_last(normed_all, val_weight).astype(jnp.bfloat16)
    lead_rows = jnp.where(has_tail, tail_rows, jnp.zeros_like(tail_rows))
    extended = jnp.concatenate([lead_rows, values], axis=0).astype(jnp.float32)
    conv_out = filters[0] * extended[TAPS - 1 : TAPS - 1 + seq_len]
    for tap in range(1, TAPS):
        conv_out = conv_out + filters[tap] * extended[TAPS - 1 - tap : TAPS - 1 - tap + seq_len]
    gate_sig = jax.nn.sigmoid(conv_out)
    gated = (conv_out * gate_sig).astype(jnp.bfloat16)
    grad_gated = contract_last(lax.all_gather(cot_rows, "tensor", axis=0, tiled=True), out_weight)
    grad_wo = contract_first(gated, lax.all_gather(cot_rows, "tensor", axis=0, tiled=True))
    grad_conv = grad_gated * gate_sig * (1.0 + conv_out * (1.0 - gate_sig))
    grad_filter = jnp.stack(
        [
            jnp.sum(grad_conv * extended[TAPS - 1 - tap : TAPS - 1 - tap + seq_len], axis=0)
            for tap in range(TAPS)
        ]
    )
    padded = jnp.pad(grad_conv, ((TAPS - 1, TAPS - 1), (0, 0)))
    grad_ext = filters[0] * padded[0 : seq_len + TAPS - 1]
    for tap in range(1, TAPS):
        grad_ext = grad_ext + filters[tap] * padded[tap : tap + seq_len + TAPS - 1]
    grad_values = grad_ext[TAPS - 1 :].astype(jnp.bfloat16)
    grad_tail = jnp.where(has_tail, grad_ext[: TAPS - 1], jnp.zeros_like(grad_ext[: TAPS - 1]))
    grad_wv = contract_first(grad_values, normed_all)
    grad_normed = lax.psum_scatter(
        jnp.dot(grad_values, val_weight, preferred_element_type=jnp.float32).astype(jnp.bfloat16),
        "tensor",
        scatter_dimension=0,
        tiled=True,
    ).astype(jnp.float32)
    gain_term = jnp.sum(grad_normed * x_float * inv_rms, axis=0)
    grad_gain = lax.psum(gain_term, "tensor")
    scaled = gain_row * grad_normed
    grad_local = (
        cot_rows.astype(jnp.float32)
        + inv_rms * scaled
        - x_float * inv_rms**3 * jnp.mean(scaled * x_float, axis=-1, keepdims=True)
    )
    received = shifted(grad_local.astype(jnp.bfloat16), "section", -1)
    return (
        received[None],
        grad_wv.astype(jnp.bfloat16)[None],
        grad_wo.astype(jnp.bfloat16)[None],
        grad_filter[None],
        grad_tail[None],
        grad_gain[None],
    )


def solution(mesh):
    placed = (
        P("section", "tensor", None),
        P("section", "tensor", None),
        P("section", None),
        P("section", "tensor", None),
        P("section", "tensor", None),
        P("section", None, "tensor"),
        P("section", None, "tensor"),
        P("section"),
    )
    return jax.shard_map(
        on_device,
        mesh=mesh,
        in_specs=placed,
        out_specs=(
            P("section", "tensor", None),
            P("section", "tensor", None),
            P("section", "tensor", None),
            P("section", None, "tensor"),
            P("section", None, "tensor"),
            P("section", None),
        ),
        check_vma=False,
    )
```

profile of v0, /device:TPU:32, one launch (start us, length us, event | category | flops | bytes accessed | tf_op | source)
XLA Modules:
  0.0 413.5 jit_solution(13749967059140600081)
XLA Ops:
  7.2 1.2 fusion.18
  8.4 1.7 fusion.20
  10.1 0.0 all-gather.6.cloned.1.call-start
  10.2 0.7 all-gather.6.cloned.1.call-update
  10.9 0.0 reduce-scatter.2.cloned.1.call-start
  11.6 0.7 fusion.27
  12.2 0.7 slice_bitcast_fusion.2
  12.9 69.8 %all-gather.4.cloned.1.call-done = bf16[512,4096]{1,0:T(8,128)(2,1)} async-done(((bf16[16,4096]{1,0:T(8,128)(2,1)}), bf16[512,4096]{1,0:T(8,128)(2,1)}) %all-gather.4.cloned.1.call-update) | async-done | bytes 4194320 | tf_op jit(solution)/shard_map/all_gather | solution.py:40
  82.7 3.4 convolution_convert_fusion.3
  86.2 0.1 multiply_add_fusion.1
  86.3 67.6 %all-gather.6.cloned.1.call-done = bf16[1,512,4096]{2,1,0:T(8,128)(2,1)} async-done(((bf16[1,16,4096]{2,1,0:T(8,128)(2,1)}), bf16[1,512,4096]{2,1,0:T(8,128)(2,1)}) %all-gather.6.cloned.1.call-update) | async-done | bytes 4194320 | tf_op jit(solution)/shard_map/all_gather | solution.py:50
  153.9 3.5 multiply_reduce_fusion.2
  157.4 0.1 multiply_add_fusion
  157.5 3.2 convolution_convert_fusion
  160.8 0.6 copy.14
  161.4 4.2 %fusion.1 = bf16[1,128,4096]{2,1,0:T(8,128)(2,1)} fusion(bf16[1,512,4096]{2,1,0:T(8,128)(2,1)} %all-gather.6.cloned.1.call-done, f32[512,128]{1,0:T(8,128)S(1)} %multiply_add_fusion.1), kind=kOutput, calls=%fused_computation.4 | convolution fusion | flops 537722880 | bytes 5505024 | tf_op jit(solution)/shard_map/dot_general | solution.py:23
  165.6 1.7 fusion
  167.3 120.2 %reduce-scatter.2.cloned.1.call-done = bf16[16,4096]{1,0:T(8,128)(2,1)} async-done(((bf16[512,4096]{1,0:T(8,128)(2,1)}), bf16[16,4096]{1,0:T(8,128)(2,1)}) %reduce-scatter.2.cloned.1.call-update) | async-done | bytes 131088 | tf_op jit(solution)/shard_map/reduce_scatter | solution.py:66
  287.6 1.2 fusion.24
  288.7 1.0 fusion.17
  289.8 7.5 %collective-permute-start = (bf16[16,4096]{1,0:T(8,128)(2,1)S(1)}, bf16[16,4096]{1,0:T(8,128)(2,1)S(1)}, u32[]{:S(2)}, u32[]{:S(2)}) collective-permute-start(bf16[16,4096]{1,0:T(8,128)(2,1)S(1)} %fusion.17), channel_id=1, source_target_pairs={{32,0},{64,32},{96,64},{128,96},{160,128},{192,160},{224,192},{256... | collective-permute-start | bytes 393224 | tf_op jit(solution)/shard_map/ppermute | solution.py:13
  297.3 0.6 fusion.26
  297.9 108.5 %psum.7 = f32[1,4096]{1,0:T(1,128)} all-reduce(f32[1,4096]{1,0:T(1,128)S(1)} %bitcast.60), channel_id=1, replica_groups=mesh['section'=16,'tensor'=32] {'tensor'}, use_global_device_ids=true, to_apply=%region_7.8 | all-reduce | flops 4096 | bytes 32768 | tf_op jit(solution)/shard_map/psum | solution.py:73
  406.3 0.7 copy.17
  (20 shorter events, 0.2 us)
Async XLA Ops:
  7.2 75.6 %copy-start = (bf16[1,128,4096]{2,1,0:T(8,128)(2,1)S(1)}, bf16[1,128,4096]{2,1,0:T(8,128)(2,1)}, u32[]{:S(2)}) copy-start(bf16[1,128,4096]{2,1,0:T(8,128)(2,1)} %param.11) | copy-start | bytes 3145732
  7.2 146.8 %copy-start.5 = (bf16[1,128,4096]{2,1,0:T(8,128)(2,1)S(1)}, bf16[1,128,4096]{2,1,0:T(8,128)(2,1)}, u32[]{:S(2)}) copy-start(bf16[1,128,4096]{2,1,0:T(8,128)(2,1)} %param.12) | copy-start | bytes 3145732
  7.2 75.5 %all-gather.4.cloned.1.call-start = ((), (), s32[]{:S(2)}) async-start(), calls=%async_computation.1 | async-start | bytes 4325376 | tf_op jit(solution)/shard_map/all_gather | solution.py:40
  10.1 143.8 %all-gather.6.cloned.1.call-start = ((), (), s32[]{:S(2)}) async-start(), calls=%async_computation.3 | async-start | bytes 4325376 | tf_op jit(solution)/shard_map/all_gather | solution.py:50
  10.9 276.7 %reduce-scatter.2.cloned.1.call-start = ((), (), s32[]{:S(2)}) async-start(), calls=%async_computation.2 | async-start | bytes 4325376 | tf_op jit(solution)/shard_map/reduce_scatter | solution.py:66
  160.8 4.8 %copy-start.1 = (bf16[512,4096]{1,0:T(8,128)(2,1)S(1)}, bf16[512,4096]{1,0:T(8,128)(2,1)}, u32[]{:S(2)}) copy-start(bf16[512,4096]{1,0:T(8,128)(2,1)} %all-gather.4.cloned.1.call-done) | copy-start | bytes 12582916
  161.3 126.2 %copy-start.2 = (bf16[1,16,4096]{2,1,0:T(8,128)(2,1)S(1)}, bf16[1,16,4096]{2,1,0:T(8,128)(2,1)}, u32[]{:S(2)}) copy-start(bf16[1,16,4096]{2,1,0:T(8,128)(2,1)} %param.8) | copy-start | bytes 393220
  161.3 126.2 %copy-start.4 = (f32[1,4096]{1,0:T(1,128)S(1)}, f32[1,4096]{1,0:T(1,128)}, u32[]{:S(2)}) copy-start(f32[1,4096]{1,0:T(1,128)} %param.10) | copy-start | bytes 49156
  165.6 123.1 %copy-start.3 = (bf16[1,16,4096]{2,1,0:T(8,128)(2,1)S(1)}, bf16[1,16,4096]{2,1,0:T(8,128)(2,1)}, u32[]{:S(2)}) copy-start(bf16[1,16,4096]{2,1,0:T(8,128)(2,1)} %param.9) | copy-start | bytes 393220
  289.8 116.6 %collective-permute-start = (bf16[16,4096]{1,0:T(8,128)(2,1)S(1)}, bf16[16,4096]{1,0:T(8,128)(2,1)S(1)}, u32[]{:S(2)}, u32[]{:S(2)}) collective-permute-start(bf16[16,4096]{1,0:T(8,128)(2,1)S(1)} %fusion.17), channel_id=1, source_target_pairs={{32,0},{64,32},{96,64},{128,96},{160,128},{192,160},{224,192},{256... | collective-permute-start | bytes 393224 | tf_op jit(solution)/shard_map/ppermute | solution.py:13
Sparse Core Ops, SparseCore 0:
  10.7 71.9 all-gather.3
  84.9 69.0 all-gather.5
  160.9 126.6 reduce-scatter.1
where the time goes:
time: 414 us
  waiting for transfers between devices  258 us (62%)
  blocking collectives  108 us (26%)
  matrix products  16.1 us (4%)
  between operations  14.5 us (4%)
  starting transfers between devices  7.63 us (2%)
  other arithmetic  6.52 us (2%)
    reduce_scatter x1, waiting for transfers between devices, on_device(): lax.psum_scatter(jnp.dot(grad_values, val_weight, preferred_element_type=...  120 us
    psum x1, blocking collectives, on_device(): grad_gain = lax.psum(gain_term, 'tensor')  108 us
    all_gather x1, waiting for transfers between devices, on_device(): normed_all = lax.all_gather(normed, 'tensor', axis=0, tiled=True)  69.8 us
    all_gather x1, waiting for transfers between devices, on_device(): lax.all_gather(cot_rows, 'tensor', axis=0, tiled=True)  67.6 us
  transfers between devices with their start and end apart: 4, of which 3 were waited for; matrix products, arithmetic and copies ran while one was open for 3% of the time, Pallas kernels for 0%

commit v1 on v0

--- a/solution.py
+++ b/solution.py
@@ -5,6 +5,11 @@
 
 TAPS = 3
 EPSILON = 1e-06
+
+
+def swapped_in(x, axis, dim):
+    sent = jnp.stack([x] * lax.axis_size(axis))
+    return jnp.concatenate(lax.all_to_all(sent, axis, 0, 0), axis=dim)
 
 
 def shifted(block, axis, distance):
@@ -47,7 +52,7 @@
         conv_out = conv_out + filters[tap] * extended[TAPS - 1 - tap : TAPS - 1 - tap + seq_len]
     gate_sig = jax.nn.sigmoid(conv_out)
     gated = (conv_out * gate_sig).astype(jnp.bfloat16)
-    grad_gated = contract_last(lax.all_gather(cot_rows, "tensor", axis=0, tiled=True), out_weight)
+    grad_gated = contract_last(swapped_in(cot_rows, "tensor", 0), out_weight)
     grad_wo = contract_first(gated, lax.all_gather(cot_rows, "tensor", axis=0, tiled=True))
     grad_conv = grad_gated * gate_sig * (1.0 + conv_out * (1.0 - gate_sig))
     grad_filter = jnp.stack(

time: 414 us -> 453 us (1.094)
  waiting for transfers between devices: 258 us -> 283 us
  starting transfers between devices: 7.63 us -> 18.2 us
    all_gather x1, waiting for transfers between devices: 69.8 us -> 98.3 us  [on_device(): normed_all = lax.all_gather(normed, 'tensor', axis=0, tiled=True)]
    all_gather x1, waiting for transfers between devices: 67.6 us -> 52.1 us  [on_device(): lax.all_gather(cot_rows, 'tensor', axis=0, tiled=True)]
    all_to_all x0 -> x1, starting transfers between devices: none -> 10.1 us  [swapped_in(): return jnp.concatenate(lax.all_to_all(sent, axis, 0, 0), axis=dim)]
    all_to_all x0 -> x1, waiting for transfers between devices: none -> 6.65 us  [swapped_in(): return jnp.concatenate(lax.all_to_all(sent, axis, 0, 0), axis=dim)]
    reduce_scatter x1, waiting for transfers between devices: 120 us -> 126 us  [on_device(): lax.psum_scatter(jnp.dot(grad_values, val_weight, preferred_element_type=...]
  transfers between devices with their start and end apart: 4 -> 5, of which waited for: 3 -> 4; matrix products, arithmetic and copies ran while one was open for 3% -> 5% of each run, Pallas kernels for 0% -> 0%
where the time goes in v1:
time: 453 us; the launch traced here: 452 us
  waiting for transfers between devices  283 us (62%)
  blocking collectives  108 us (24%)
  starting transfers between devices  18.2 us (4%)
  matrix products  18 us (4%)
  between operations  14.5 us (3%)
  other arithmetic  5.8 us (1%)
  local copies, waits for them, and re-layouts  4.63 us (1%)
    reduce_scatter x1, waiting for transfers between devices, on_device(): lax.psum_scatter(jnp.dot(grad_values, val_weight, preferred_element_type=...  126 us
    psum x1, blocking collectives, on_device(): grad_gain = lax.psum(gain_term, 'tensor')  108 us
    all_gather x1, waiting for transfers between devices, on_device(): normed_all = lax.all_gather(normed, 'tensor', axis=0, tiled=True)  98.3 us
    all_gather x1, waiting for transfers between devices, on_device(): lax.all_gather(cot_rows, 'tensor', axis=0, tiled=True)  52.1 us
    all_to_all x1, starting transfers between devices, swapped_in(): return jnp.concatenate(lax.all_to_all(sent, axis, 0, 0), axis=dim)  10.1 us
  transfers between devices with their start and end apart: 5, of which 4 were waited for; matrix products, arithmetic and copies ran while one was open for 5% of the time, Pallas kernels for 0%

profile of v1, /device:TPU:32, one launch (start us, length us, event | category | flops | bytes accessed | tf_op | source)
XLA Modules:
  0.0 452.3 jit_solution(11367107334244772959)
XLA Ops:
  7.2 1.1 fusion.11
  8.4 1.7 fusion.13
  10.1 3.4 stack.15
  13.4 10.1 %all-to-all-start = ((bf16[32,16,4096]{2,1,0:T(8,128)(2,1)}), bf16[32,16,4096]{2,1,0:T(8,128)(2,1)}, u32[]{:S(2)}, u32[]{:S(2)}) async-start(bf16[32,16,4096]{2,1,0:T(8,128)(2,1)} %stack.15), calls=%async_computation | async-start | bytes 8388608 | tf_op jit(solution)/shard_map/all_to_all | solution.py:12
  23.6 0.0 all-gather.6.cloned.1.call-start
  23.6 0.7 all-gather.6.cloned.1.call-update
  25.1 98.3 %all-gather.4.cloned.1.call-done = bf16[512,4096]{1,0:T(8,128)(2,1)} async-done(((bf16[16,4096]{1,0:T(8,128)(2,1)}), bf16[512,4096]{1,0:T(8,128)(2,1)}) %all-gather.4.cloned.1.call-update) | async-done | bytes 4194320 | tf_op jit(solution)/shard_map/all_gather | solution.py:45
  123.4 3.4 convolution_convert_fusion.3
  126.8 0.1 multiply_add_fusion.1
  126.9 6.6 %all-to-all-done = bf16[32,16,4096]{2,1,0:T(8,128)(2,1)} async-done(((bf16[32,16,4096]{2,1,0:T(8,128)(2,1)}), bf16[32,16,4096]{2,1,0:T(8,128)(2,1)}, u32[]{:S(2)}, u32[]{:S(2)}) %all-to-all-start) | async-done | bytes 4194336 | tf_op jit(solution)/shard_map/all_to_all | solution.py:12
  133.6 3.5 multiply_reduce_fusion.2
  137.1 0.1 multiply_add_fusion
  137.2 3.2 convolution_convert_fusion
  140.4 0.6 copy.14
  141.0 3.9 fusion
  144.9 52.1 %all-gather.6.cloned.1.call-done = bf16[1,512,4096]{2,1,0:T(8,128)(2,1)} async-done(((bf16[1,16,4096]{2,1,0:T(8,128)(2,1)}), bf16[1,512,4096]{2,1,0:T(8,128)(2,1)}) %all-gather.6.cloned.1.call-update) | async-done | bytes 4194320 | tf_op jit(solution)/shard_map/all_gather | solution.py:56
  197.0 3.9 fusion.1
  200.9 125.6 %reduce-scatter.2.cloned.1.call-done = bf16[16,4096]{1,0:T(8,128)(2,1)} async-done(((bf16[512,4096]{1,0:T(8,128)(2,1)}), bf16[16,4096]{1,0:T(8,128)(2,1)}) %reduce-scatter.2.cloned.1.call-update) | async-done | bytes 131088 | tf_op jit(solution)/shard_map/reduce_scatter | solution.py:71
  326.6 1.2 fusion.17
  327.8 1.0 fusion.10
  328.8 7.9 %collective-permute-start = (bf16[16,4096]{1,0:T(8,128)(2,1)S(1)}, bf16[16,4096]{1,0:T(8,128)(2,1)S(1)}, u32[]{:S(2)}, u32[]{:S(2)}) collective-permute-start(bf16[16,4096]{1,0:T(8,128)(2,1)S(1)} %fusion.10), channel_id=1, source_target_pairs={{32,0},{64,32},{96,64},{128,96},{160,128},{192,160},{224,192},{256... | collective-permute-start | bytes 393224 | tf_op jit(solution)/shard_map/ppermute | solution.py:18
  336.7 0.6 fusion.19
  337.3 107.8 %psum.7 = f32[1,4096]{1,0:T(1,128)} all-reduce(f32[1,4096]{1,0:T(1,128)S(1)} %bitcast.54), channel_id=1, replica_groups=mesh['section'=16,'tensor'=32] {'tensor'}, use_global_device_ids=true, to_apply=%region_7.8 | all-reduce | flops 4096 | bytes 32768 | tf_op jit(solution)/shard_map/psum | solution.py:78
  445.1 0.7 copy.17
  (25 shorter events, 0.2 us)
Async XLA Ops:
  7.2 116.2 %copy-start = (bf16[1,128,4096]{2,1,0:T(8,128)(2,1)S(1)}, bf16[1,128,4096]{2,1,0:T(8,128)(2,1)}, u32[]{:S(2)}) copy-start(bf16[1,128,4096]{2,1,0:T(8,128)(2,1)} %param.11) | copy-start | bytes 3145732
  7.2 116.2 %all-gather.4.cloned.1.call-start = ((), (), s32[]{:S(2)}) async-start(), calls=%async_computation.2 | async-start | bytes 4325376 | tf_op jit(solution)/shard_map/all_gather | solution.py:45
  13.4 11.6 %copy-start.6 = (bf16[1,2,128]{2,1,0:T(2,128)(2,1)S(1)}, bf16[1,2,128]{2,1,0:T(2,128)(2,1)}, u32[]{:S(2)}) copy-start(bf16[1,2,128]{2,1,0:T(2,128)(2,1)} %param.14) | copy-start | bytes 1540
  13.4 11.6 %copy-start.4 = (f32[1,3,128]{2,0,1:T(1,128)S(1)}, f32[1,3,128]{2,0,1:T(1,128)}, u32[]{:S(2)}) copy-start(f32[1,3,128]{2,0,1:T(1,128)} %param.13) | copy-start | bytes 4612
  13.4 120.1 %all-to-all-start = ((bf16[32,16,4096]{2,1,0:T(8,128)(2,1)}), bf16[32,16,4096]{2,1,0:T(8,128)(2,1)}, u32[]{:S(2)}, u32[]{:S(2)}) async-start(bf16[32,16,4096]{2,1,0:T(8,128)(2,1)} %stack.15), calls=%async_computation | async-start | bytes 8388608 | tf_op jit(solution)/shard_map/all_to_all | solution.py:12
  23.6 110.0 %copy-start.5 = (bf16[1,128,4096]{2,1,0:T(8,128)(2,1)S(1)}, bf16[1,128,4096]{2,1,0:T(8,128)(2,1)}, u32[]{:S(2)}) copy-start(bf16[1,128,4096]{2,1,0:T(8,128)(2,1)} %param.12) | copy-start | bytes 3145732
  23.6 173.4 %all-gather.6.cloned.1.call-start = ((), (), s32[]{:S(2)}) async-start(), calls=%async_computation.4 | async-start | bytes 4325376 | tf_op jit(solution)/shard_map/all_gather | solution.py:56
  24.3 302.2 %reduce-scatter.2.cloned.1.call-start = ((), (), s32[]{:S(2)}) async-start(), calls=%async_computation.3 | async-start | bytes 4325376 | tf_op jit(solution)/shard_map/reduce_scatter | solution.py:71
  141.0 185.6 %copy-start.1 = (bf16[1,16,4096]{2,1,0:T(8,128)(2,1)S(1)}, bf16[1,16,4096]{2,1,0:T(8,128)(2,1)}, u32[]{:S(2)}) copy-start(bf16[1,16,4096]{2,1,0:T(8,128)(2,1)} %param.8) | copy-start | bytes 393220
  141.0 185.6 %copy-start.3 = (f32[1,4096]{1,0:T(1,128)S(1)}, f32[1,4096]{1,0:T(1,128)}, u32[]{:S(2)}) copy-start(f32[1,4096]{1,0:T(1,128)} %param.10) | copy-start | bytes 49156
  144.9 182.8 %copy-start.2 = (bf16[1,16,4096]{2,1,0:T(8,128)(2,1)S(1)}, bf16[1,16,4096]{2,1,0:T(8,128)(2,1)}, u32[]{:S(2)}) copy-start(bf16[1,16,4096]{2,1,0:T(8,128)(2,1)} %param.9) | copy-start | bytes 393220
  328.8 116.3 %collective-permute-start = (bf16[16,4096]{1,0:T(8,128)(2,1)S(1)}, bf16[16,4096]{1,0:T(8,128)(2,1)S(1)}, u32[]{:S(2)}, u32[]{:S(2)}) collective-permute-start(bf16[16,4096]{1,0:T(8,128)(2,1)S(1)} %fusion.10), channel_id=1, source_target_pairs={{32,0},{64,32},{96,64},{128,96},{160,128},{192,160},{224,192},{256... | collective-permute-start | bytes 393224 | tf_op jit(solution)/shard_map/ppermute | solution.py:18
Sparse Core Ops, SparseCore 0:
  10.7 112.5 all-gather.3
  125.5 71.4 all-gather.5
  199.8 126.7 reduce-scatter.1
